TPU v7x, 256 devices: a whole 4x4x8 slice. The times are simulated.
256 devices in a mesh: batch: 16 (over z, core), proto: 16 (over x, y).
Axes of the slice: x: 4, y: 4, z: 8, core: 2. Of those that a mesh axis runs over, the one named last changes fastest.
Arguments:
- slow_embed: bfloat16 [16384, 256], P('batch'), may hold values from -1 to 1
- fast_embed: bfloat16 [16384, 256], P('batch'), may hold values from -1 to 1
- prototypes: float32 [32768, 256], P('proto'), may hold values from -1 to 1
Outputs:
- proto_grad: float32 [32768, 256], P('proto')
- slow_grad: float32 [16384, 256], P('batch')
- fast_grad: float32 [16384, 256], P('batch')
All inputs are finite; a program needn't handle non-finite values.
Results may differ from a plain program's by a relative error of at most 0.0005.
The roundings to bfloat16 on the way count: a program that leaves them out, or rounds other values in their place, can miss the bound.
Values sent between devices are 32-bit elements; how exact they have to be, the bound alone decides.
A program may use at most 128 MiB of HBM per device.

v0:
```python
import jax
import jax.numpy as jnp
from jax import lax
from jax.sharding import PartitionSpec as P

ITERS = 3
CODE_EPS = 0.05
TEMPER = 0.1
NORM_EPS = 1e-06


def normalize(raw_rows):
    lengths = jnp.sqrt(jnp.sum(raw_rows * raw_rows, axis=-1, keepdims=True) + 1e-12)
    return (raw_rows / lengths, lengths)


def project_back(grad_unit, unit_vec, lengths):
    along = jnp.sum(unit_vec * grad_unit, axis=-1, keepdims=True)
    return (grad_unit - unit_vec * along) / lengths


def row_total(row_terms):
    return lax.psum(row_terms, "proto")


def normalizers(proto_square, embed_square, proto_entries, embed_entries):
    totals = lax.psum((proto_square, embed_square), ("batch", "proto"))
    proto_factor = lax.rsqrt(totals[0] / proto_entries + NORM_EPS)
    embed_factor = lax.rsqrt(totals[1] / embed_entries + NORM_EPS)
    return (proto_factor, embed_factor)


def body(slow_embed, fast_embed, prototypes):
    clip_dev = slow_embed.shape[0]
    proto_dev = prototypes.shape[0]
    feat_width = prototypes.shape[1]
    batch_count = lax.axis_size("batch")
    proto_count = lax.axis_size("proto")
    clips_all = clip_dev * batch_count
    protos_all = proto_dev * proto_count
    proto_entries = float(protos_all * feat_width)
    embed_entries = float(2 * clips_all * feat_width)
    raw_views = jnp.stack([slow_embed, fast_embed]).astype(jnp.float32)
    unit_vec, lengths = normalize(raw_views)
    unit_b = unit_vec.astype(jnp.bfloat16)
    proto_unit, proto_len = normalize(prototypes)
    proto_b = proto_unit.astype(jnp.bfloat16)
    scores = jnp.einsum("vbd,kd->vbk", unit_b, proto_b, preferred_element_type=jnp.float32)
    code_table = jnp.exp(scores / CODE_EPS)
    soft_exp = jnp.exp(scores / TEMPER)
    denom_terms = jnp.sum(soft_exp, axis=2)
    denominator = lax.psum(denom_terms, "proto")
    clip_scale = jnp.ones((2, clip_dev), jnp.float32)
    for iteration in range(ITERS):
        col_total = lax.psum(jnp.sum(code_table * clip_scale[:, :, None], axis=1), "batch")
        proto_scale = 1.0 / (protos_all * col_total)
        row_terms = jnp.sum(code_table * proto_scale[:, None, :], axis=2)
        if iteration == 0:
            clip_total = row_total(row_terms)
        else:
            clip_total = row_total(row_terms)
        clip_scale = 1.0 / (clips_all * clip_total)
    codes = code_table * proto_scale[:, None, :] / clip_total[:, :, None]
    probs = soft_exp / denominator[:, :, None]
    score_grad = (jnp.stack([probs[0] - codes[1], probs[1] - codes[0]]) / TEMPER).astype(
        jnp.bfloat16
    )
    proto_terms = jnp.einsum("vbk,vbd->kd", score_grad, unit_b, preferred_element_type=jnp.float32)
    grad_proto_unit = lax.psum(proto_terms, "batch")
    embed_terms = jnp.einsum("vbk,kd->vbd", score_grad, proto_b, preferred_element_type=jnp.float32)
    grad_unit = lax.psum(embed_terms, "proto")
    grad_proto = project_back(grad_proto_unit, proto_unit, proto_len)
    grad_embed = project_back(grad_unit, unit_vec, lengths)
    proto_factor, embed_factor = normalizers(
        jnp.sum(grad_proto * grad_proto) / batch_count,
        jnp.sum(grad_embed * grad_embed) / proto_count,
        proto_entries,
        embed_entries,
    )
    proto_grad = grad_proto * proto_factor
    slow_grad = grad_embed[0] * embed_factor
    fast_grad = grad_embed[1] * embed_factor
    return (proto_grad, slow_grad, fast_grad)


def solution(mesh):
    placed = (P("batch", None), P("batch", None), P("proto", None))
    return jax.shard_map(
        body,
        mesh=mesh,
        in_specs=placed,
        out_specs=(P("proto", None), P("batch", None), P("batch", None)),
        check_vma=False,
    )
```

profile of v0, /device:TPU:1, one launch (start us, length us, event | category | flops | bytes accessed | tf_op | source)
XLA Modules:
  0.0 716.6 jit_solution(129335976540485152)
XLA Ops:
  8.8 1.9 multiply_reduce_fusion.9
  10.7 9.2 %fusion.4 = (f32[2,2048]{1,0:T(2,128)S(1)}, f32[2,1024,2048]{2,1,0:T(8,128)}) fusion(f32[2048,256]{1,0:T(8,128)} %param.5, f32[2048]{0:T(1024)S(1)} %add_sqrt_fusion, f32[2,1024]{1,0:T(2,128)S(1)} %add_sqrt_fusion.1, bf16[1,1024,256]{2,1,0:T(8,128)(2,1)} %bitcast.16, bf16[1,1024,256]{2,1,0:T(8,128)(2,1)} %bitcast.20), kind=kOutput, calls=%fused_computation.15 | convolution fusion | flops 2159013888 | bytes 19955712 | tf_op jit(solution)/shard_map/vbd,kd->vbk/dot_general | solution.py:48
  20.0 48.8 %psum.78 = f32[2,2048]{1,0:T(2,128)S(1)} all-reduce(f32[2,2048]{1,0:T(2,128)S(1)} %get-tuple-element.17), channel_id=1, replica_groups=mesh['batch'=16,'proto'=16] {'batch'}, use_global_device_ids=true, to_apply=%region_5.0 | all-reduce | flops 4096 | bytes 32768 | tf_op jit(solution)/shard_map/psum | solution.py:55
  68.8 9.0 %fusion.3 = (f32[2,1024]{1,0:T(2,128)S(1)}, f32[2,1024]{1,0:T(2,128)S(1)}) fusion(f32[2,1024,2048]{2,1,0:T(8,128)} %get-tuple-element.18, f32[2,2048]{1,0:T(2,128)S(1)} %multiply_divide_fusion.3), kind=kLoop, calls=%fused_computation.12 | loop fusion | flops 20967424 | bytes 16809984 | tf_op jit(solution)/shard_map/reduce_sum | solution.py:51
  77.8 34.0 %psum.79 = f32[2,1024]{1,0:T(2,128)S(1)} all-reduce(f32[2,1024]{1,0:T(2,128)S(1)} %get-tuple-element.4), channel_id=1, replica_groups=mesh['batch'=16,'proto'=16] {'proto'}, use_global_device_ids=true, to_apply=%region_7.0 | all-reduce | flops 2048 | bytes 16384 | tf_op jit(solution)/shard_map/psum | solution.py:23
  111.8 7.4 %multiply_reduce_fusion.2 = f32[2,2048]{1,0:T(2,128)S(1)} fusion(f32[2,1024]{1,0:T(2,128)S(1)} %multiply_divide_fusion.5, f32[2,1024,2048]{2,1,0:T(8,128)} %get-tuple-element.18), kind=kLoop, calls=%fused_computation.5 | loop fusion | flops 12578816 | bytes 16801792 | tf_op jit(solution)/shard_map/reduce_sum | solution.py:55
  119.1 52.9 %psum.80 = f32[2,2048]{1,0:T(2,128)S(1)} all-reduce(f32[2,2048]{1,0:T(2,128)S(1)} %multiply_reduce_fusion.2), channel_id=1, replica_groups=mesh['batch'=16,'proto'=16] {'batch'}, use_global_device_ids=true, to_apply=%region_9.0 | all-reduce | flops 4096 | bytes 32768 | tf_op jit(solution)/shard_map/psum | solution.py:55
  172.0 8.6 %multiply_reduce_fusion.1 = f32[2,1024]{1,0:T(2,128)S(1)} fusion(f32[2,2048]{1,0:T(2,128)S(1)} %multiply_divide_fusion.2, f32[2,1024,2048]{2,1,0:T(8,128)} %get-tuple-element.18), kind=kLoop, calls=%fused_computation.4 | loop fusion | flops 12580864 | bytes 16801792 | tf_op jit(solution)/shard_map/reduce_sum | solution.py:57
  180.6 29.0 %psum.81 = f32[2,1024]{1,0:T(2,128)S(1)} all-reduce(f32[2,1024]{1,0:T(2,128)S(1)} %multiply_reduce_fusion.1), channel_id=1, replica_groups=mesh['batch'=16,'proto'=16] {'proto'}, use_global_device_ids=true, to_apply=%region_11.0 | all-reduce | flops 2048 | bytes 16384 | tf_op jit(solution)/shard_map/psum | solution.py:23
  209.7 7.4 %multiply_reduce_fusion = f32[2,2048]{1,0:T(2,128)S(1)} fusion(f32[2,1024]{1,0:T(2,128)S(1)} %multiply_divide_fusion.4, f32[2,1024,2048]{2,1,0:T(8,128)} %get-tuple-element.18), kind=kLoop, calls=%fused_computation.3 | loop fusion | flops 12578816 | bytes 16801792 | tf_op jit(solution)/shard_map/reduce_sum | solution.py:55
  217.0 52.8 %psum.82 = f32[2,2048]{1,0:T(2,128)S(1)} all-reduce(f32[2,2048]{1,0:T(2,128)S(1)} %multiply_reduce_fusion), channel_id=1, replica_groups=mesh['batch'=16,'proto'=16] {'batch'}, use_global_device_ids=true, to_apply=%region_13.0 | all-reduce | flops 4096 | bytes 32768 | tf_op jit(solution)/shard_map/psum | solution.py:55
  269.9 8.6 %multiply_reduce_fusion.4 = f32[2,1024]{1,0:T(2,128)S(1)} fusion(f32[2,2048]{1,0:T(2,128)S(1)} %multiply_divide_fusion.1, f32[2,1024,2048]{2,1,0:T(8,128)} %get-tuple-element.18), kind=kLoop, calls=%fused_computation.10 | loop fusion | flops 12580864 | bytes 16801792 | tf_op jit(solution)/shard_map/reduce_sum | solution.py:57
  278.5 57.5 %all-reduce.1 = (f32[2,1024]{1,0:T(2,128)S(1)}, f32[2,1024]{1,0:T(2,128)S(1)}) all-reduce(f32[2,1024]{1,0:T(2,128)S(1)} %multiply_reduce_fusion.4, f32[2,1024]{1,0:T(2,128)S(1)} %get-tuple-element.3), channel_id=1, replica_groups=mesh['batch'=16,'proto'=16] {'proto'}, use_global_device_ids=true, to_apply=%region_15.0 | all-reduce | flops 4096 | bytes 32768 | tf_op jit(solution)/shard_map/psum | solution.py:23
  336.0 18.3 %fusion.2 = (f32[2,1024,2048]{2,1,0:T(8,128)}, f32[2,1024,2048]{2,1,0:T(8,128)}) fusion(f32[2,1024,2048]{2,1,0:T(8,128)} %get-tuple-element.18, f32[2,1024]{1,0:T(2,128)S(1)} %get-tuple-element.8, f32[2,1024]{1,0:T(2,128)S(1)} %get-tuple-element.7, f32[2,2048]{1,0:T(2,128)S(1)} %multiply_divide_fusion.1), kind=kLoop, calls=%fused_computation.11 | loop fusion | flops 20971520 | bytes 50364416 | tf_op jit(solution)/shard_map/div | solution.py:64
  354.3 19.2 %slice_subtract_fusion.1 = (f32[1,1024,2048]{2,1,0:T(8,128)}, f32[1,1024,2048]{2,1,0:T(8,128)}) fusion(f32[2,1024,2048]{2,1,0:T(8,128)} %get-tuple-element.14, f32[2,1024,2048]{2,1,0:T(8,128)} %get-tuple-element.13), kind=kLoop, calls=%fused_computation.14 | loop fusion | flops 4194304 | bytes 50331648 | tf_op jit(solution)/shard_map/sub | solution.py:65
  373.5 8.8 %convolution_bitcast_fusion = f32[2048,256]{1,0:T(8,128)} fusion(f32[1,1024,2048]{2,1,0:T(8,128)} %get-tuple-element.12, f32[1,1024,2048]{2,1,0:T(8,128)} %get-tuple-element.11, f32[2,1024]{1,0:T(2,128)S(1)} %add_sqrt_fusion.1, bf16[1,1024,256]{2,1,0:T(8,128)(2,1)S(1)} %bitcast.17, bf16[1,1024,256]{2,1,0:T(8,128)(2,1)S(1)} %bitcast.21), kind=kOutput, calls=%fused_computation.16 | convolution fusion | flops 2162163712 | bytes 19931136 | tf_op jit(solution)/shard_map/vbk,vbd->kd/dot_general | solution.py:68
  382.6 8.5 %fusion.11 = f32[2,1024,256]{2,1,0:T(8,128)} fusion(f32[1,1024,2048]{2,1,0:T(8,128)} %get-tuple-element.12, f32[1,1024,2048]{2,1,0:T(8,128)} %get-tuple-element.11, f32[2048,256]{1,0:T(8,128)S(1)} %copy-done, f32[2048]{0:T(1024)S(1)} %add_sqrt_fusion), kind=kOutput, calls=%fused_computation.33 | convolution fusion | flops 2161115136 | bytes 20979712 | tf_op jit(solution)/shard_map/vbk,kd->vbd/dot_general | solution.py:70
  391.2 116.1 %all-reduce.5.cloned.1.call-done = f32[2048,256]{1,0:T(8,128)} async-done(((f32[2048,256]{1,0:T(8,128)}), f32[2048,256]{1,0:T(8,128)}) %all-reduce.5.cloned.1.call-update) | async-done | bytes 2097168 | tf_op jit(solution)/shard_map/psum | solution.py:69
  507.3 2.2 multiply_reduce_fusion.8
  509.5 3.6 multiply_reduce_fusion.7
  513.8 97.2 %all-reduce.7.cloned.1.call-done = f32[2,1024,256]{2,1,0:T(8,128)} async-done(((f32[2,1024,256]{2,1,0:T(8,128)}), f32[2,1024,256]{2,1,0:T(8,128)}) %all-reduce.7.cloned.1.call-update) | async-done | bytes 2097168 | tf_op jit(solution)/shard_map/psum | solution.py:71
  611.0 15.5 %multiply_reduce_fusion.5 = (f32[]{:T(128)}, f32[2,1024,256]{2,1,0:T(8,128)}) fusion(f32[2,1024,256]{2,1,0:T(8,128)} %all-reduce.7.cloned.1.call-done, f32[2,1024]{1,0:T(2,128)S(1)} %add_sqrt_fusion.1, bf16[1,1024,256]{2,1,0:T(8,128)(2,1)S(1)} %bitcast.18, bf16[1,1024,256]{2,1,0:T(8,128)(2,1)S(1)} %bitcast.22), kind=kOutput, calls=%fused_computation.20 | output fusion | flops 7342334 | bytes 5251076 | tf_op jit(solution)/shard_map/mul | solution.py:19
  627.1 76.8 %all-reduce = (f32[]{:T(128)}, f32[]{:T(128)}) all-reduce(f32[]{:T(128)S(6)} %div.101, f32[]{:T(128)S(6)} %div.104), channel_id=1, replica_groups=mesh['batch'=16,'proto'=16] {'batch','proto'}, use_global_device_ids=true, to_apply=%region_19.0 | all-reduce | flops 2 | bytes 16 | tf_op jit(solution)/shard_map/psum | solution.py:27
  706.8 3.0 fusion.9
  (21 shorter events, 3.5 us)
Async XLA Ops:
  7.2 500.1 %all-reduce.5.cloned.1.call-start = ((), (), s32[]{:S(2)}) async-start(), calls=%async_computation | async-start | bytes 4194304 | tf_op jit(solution)/shard_map/psum | solution.py:69
  354.3 19.2 %copy-start.2 = (bf16[1024,256]{1,0:T(8,128)(2,1)S(1)}, bf16[1024,256]{1,0:T(8,128)(2,1)}, u32[]{:S(2)}) copy-start(bf16[1024,256]{1,0:T(8,128)(2,1)} %param.4) | copy-start | bytes 1572868
  354.3 19.2 %copy-start.3 = (bf16[1024,256]{1,0:T(8,128)(2,1)S(1)}, bf16[1024,256]{1,0:T(8,128)(2,1)}, u32[]{:S(2)}) copy-start(bf16[1024,256]{1,0:T(8,128)(2,1)} %param.3) | copy-start | bytes 1572868
  373.5 9.1 %copy-start = (f32[2048,256]{1,0:T(8,128)S(1)}, f32[2048,256]{1,0:T(8,128)}, u32[]{:S(2)}) copy-start(f32[2048,256]{1,0:T(8,128)} %param.5) | copy-start | bytes 6291460
  382.3 228.7 %all-reduce.7.cloned.1.call-start = ((), (), s32[]{:S(2)}) async-start(), calls=%async_computation.1 | async-start | bytes 4194304 | tf_op jit(solution)/shard_map/psum | solution.py:71
  513.8 191.5 %copy-start.1 = (f32[2048,256]{1,0:T(8,128)S(1)}, f32[2048,256]{1,0:T(8,128)}, u32[]{:S(2)}) copy-start(f32[2048,256]{1,0:T(8,128)} %get-tuple-element.10) | copy-start | bytes 6291460
Sparse Core Ops, SparseCore 0:
  382.4 124.8 all-reduce.4
  510.6 100.3 all-reduce.6
where the time goes:
time: 717 us
  blocking collectives  352 us (49%)
  waiting for transfers between devices  213 us (30%)
  other arithmetic  108 us (15%)
  matrix products  26.5 us (4%)
  between operations  16.9 us (2%)
    psum x3, blocking collectives, body(): lax.psum(jnp.sum(code_table * clip_scale[:, :, None], axis=1), 'batch')  155 us
    psum x3, blocking collectives, row_total(): return lax.psum(row_terms, 'proto')  121 us
    psum x1, waiting for transfers between devices, body(): grad_proto_unit = lax.psum(proto_terms, 'batch')  116 us
    psum x1, waiting for transfers between devices, body(): grad_unit = lax.psum(embed_terms, 'proto')  97.2 us
    psum x1, blocking collectives, normalizers(): totals = lax.psum((proto_square, embed_square), ('batch', 'proto'))  76.8 us
    sub x1, other arithmetic, body(): probs[0] - codes[1]  19.2 us
    div x1, other arithmetic, body(): probs = soft_exp / denominator[:, :, None]  18.3 us
    reduce_sum x2, other arithmetic, body(): row_terms = jnp.sum(code_table * proto_scale[:, None, :], axis=2)  17.2 us
  transfers between devices with their start and end apart: 2, of which 2 were waited for; matrix products, arithmetic and copies ran while one was open for 2% of the time, Pallas kernels for 0%

commit v1 on v0

--- a/solution.py
+++ b/solution.py
@@ -68,7 +68,11 @@
     proto_terms = jnp.einsum("vbk,vbd->kd", score_grad, unit_b, preferred_element_type=jnp.float32)
     grad_proto_unit = lax.psum(proto_terms, "batch")
     embed_terms = jnp.einsum("vbk,kd->vbd", score_grad, proto_b, preferred_element_type=jnp.float32)
-    grad_unit = lax.psum(embed_terms, "proto")
+    grad_unit = embed_terms
+    for hop in (1, 2, 4, 8):
+        grad_unit = grad_unit + lax.ppermute(
+            grad_unit, "proto", [(dev, dev ^ hop) for dev in range(16)]
+        )
     grad_proto = project_back(grad_proto_unit, proto_unit, proto_len)
     grad_embed = project_back(grad_unit, unit_vec, lengths)
     proto_factor, embed_factor = normalizers(

time: 717 us -> 749 us (1.045)
  waiting for transfers between devices: 213 us -> 243 us
  other arithmetic: 108 us -> 100 us
  starting transfers between devices: 0.3 us -> 7.97 us
    psum x1 -> x0, waiting for transfers between devices: 97.2 us -> none  [body(): grad_unit = lax.psum(embed_terms, 'proto')]
    ppermute x0 -> x4, waiting for transfers between devices: none -> 96.2 us  [body(): lax.ppermute(grad_unit, 'proto', [(dev, dev ^ hop) for dev in range(16)])]
    psum x1, waiting for transfers between devices: 116 us -> 147 us  [body(): grad_proto_unit = lax.psum(proto_terms, 'batch')]
    mul x1, other arithmetic: 15.5 us -> 6.62 us  [project_back(): return (grad_unit - unit_vec * along) / lengths]
    ppermute x0 -> x4, starting transfers between devices: none -> 7.93 us  [body(): lax.ppermute(grad_unit, 'proto', [(dev, dev ^ hop) for dev in range(16)])]
  transfers between devices with their start and end apart: 2 -> 5, of which waited for: 2 -> 4; matrix products, arithmetic and copies ran while one was open for 2% -> 1% of each run, Pallas kernels for 0% -> 0%
where the time goes in v1:
time: 749 us; the launch traced here: 748 us
  blocking collectives  353 us (47%)
  waiting for transfers between devices  243 us (32%)
  other arithmetic  100 us (13%)
  matrix products  20.7 us (3%)
  between operations  17.1 us (2%)
  starting transfers between devices  7.97 us (1%)
    psum x3, blocking collectives, body(): lax.psum(jnp.sum(code_table * clip_scale[:, :, None], axis=1), 'batch')  155 us
    psum x1, waiting for transfers between devices, body(): grad_proto_unit = lax.psum(proto_terms, 'batch')  147 us
    psum x3, blocking collectives, row_total(): return lax.psum(row_terms, 'proto')  121 us
    ppermute x4, waiting for transfers between devices, body(): lax.ppermute(grad_unit, 'proto', [(dev, dev ^ hop) for dev in range(16)])  96.2 us
    psum x1, blocking collectives, normalizers(): totals = lax.psum((proto_square, embed_square), ('batch', 'proto'))  77.9 us
    sub x1, other arithmetic, body(): probs[0] - codes[1]  19.2 us
    div x1, other arithmetic, body(): probs = soft_exp / denominator[:, :, None]  18.3 us
    reduce_sum x2, other arithmetic, body(): row_terms = jnp.sum(code_table * proto_scale[:, None, :], axis=2)  17.2 us
  transfers between devices with their start and end apart: 5, of which 4 were waited for; matrix products, arithmetic and copies ran while one was open for 1% of the time, Pallas kernels for 0%

profile of v1, /device:TPU:1, one launch (start us, length us, event | category | flops | bytes accessed | tf_op | source)
XLA Modules:
  0.0 748.4 jit_solution(7811103556797707655)
XLA Ops:
  11.9 9.2 %fusion.4 = (f32[2,2048]{1,0:T(2,128)S(1)}, f32[2,1024,2048]{2,1,0:T(8,128)}) fusion(f32[2048,256]{1,0:T(8,128)} %param.5, f32[2048]{0:T(1024)S(1)} %add_sqrt_fusion, f32[2,1024]{1,0:T(2,128)S(1)} %add_sqrt_fusion.1, bf16[1,1024,256]{1,2,0:T(8,128)(2,1)S(1)} %bitcast.25, bf16[1,1024,256]{1,2,0:T(8,128)(2,1)S(1)} %bitcast.21), kind=kOutput, calls=%fused_computation.15 | convolution fusion | flops 2159013888 | bytes 19955712 | tf_op jit(solution)/shard_map/vbd,kd->vbk/dot_general | solution.py:48
  21.2 48.8 %psum.71 = f32[2,2048]{1,0:T(2,128)S(1)} all-reduce(f32[2,2048]{1,0:T(2,128)S(1)} %get-tuple-element.20), channel_id=1, replica_groups=mesh['batch'=16,'proto'=16] {'batch'}, use_global_device_ids=true, to_apply=%region_5.0 | all-reduce | flops 4096 | bytes 32768 | tf_op jit(solution)/shard_map/psum | solution.py:55
  70.0 9.0 %fusion.3 = (f32[2,1024]{1,0:T(2,128)S(1)}, f32[2,1024]{1,0:T(2,128)S(1)}) fusion(f32[2,1024,2048]{2,1,0:T(8,128)} %get-tuple-element.21, f32[2,2048]{1,0:T(2,128)S(1)} %multiply_divide_fusion.3), kind=kLoop, calls=%fused_computation.12 | loop fusion | flops 20967424 | bytes 16809984 | tf_op jit(solution)/shard_map/reduce_sum | solution.py:51
  79.0 34.0 %psum.72 = f32[2,1024]{1,0:T(2,128)S(1)} all-reduce(f32[2,1024]{1,0:T(2,128)S(1)} %get-tuple-element.7), channel_id=1, replica_groups=mesh['batch'=16,'proto'=16] {'proto'}, use_global_device_ids=true, to_apply=%region_7.0 | all-reduce | flops 2048 | bytes 16384 | tf_op jit(solution)/shard_map/psum | solution.py:23
  113.0 7.4 multiply_reduce_fusion.2
  120.3 52.9 %psum.73 = f32[2,2048]{1,0:T(2,128)S(1)} all-reduce(f32[2,2048]{1,0:T(2,128)S(1)} %multiply_reduce_fusion.2), channel_id=1, replica_groups=mesh['batch'=16,'proto'=16] {'batch'}, use_global_device_ids=true, to_apply=%region_9.0 | all-reduce | flops 4096 | bytes 32768 | tf_op jit(solution)/shard_map/psum | solution.py:55
  173.3 8.6 %multiply_reduce_fusion.1 = f32[2,1024]{1,0:T(2,128)S(1)} fusion(f32[2,2048]{1,0:T(2,128)S(1)} %multiply_divide_fusion.2, f32[2,1024,2048]{2,1,0:T(8,128)} %get-tuple-element.21), kind=kLoop, calls=%fused_computation.4 | loop fusion | flops 12580864 | bytes 16801792 | tf_op jit(solution)/shard_map/reduce_sum | solution.py:57
  181.9 29.0 %psum.74 = f32[2,1024]{1,0:T(2,128)S(1)} all-reduce(f32[2,1024]{1,0:T(2,128)S(1)} %multiply_reduce_fusion.1), channel_id=1, replica_groups=mesh['batch'=16,'proto'=16] {'proto'}, use_global_device_ids=true, to_apply=%region_11.0 | all-reduce | flops 2048 | bytes 16384 | tf_op jit(solution)/shard_map/psum | solution.py:23
  210.9 7.4 multiply_reduce_fusion
  218.3 52.8 %psum.75 = f32[2,2048]{1,0:T(2,128)S(1)} all-reduce(f32[2,2048]{1,0:T(2,128)S(1)} %multiply_reduce_fusion), channel_id=1, replica_groups=mesh['batch'=16,'proto'=16] {'batch'}, use_global_device_ids=true, to_apply=%region_13.0 | all-reduce | flops 4096 | bytes 32768 | tf_op jit(solution)/shard_map/psum | solution.py:55
  271.1 8.6 %multiply_reduce_fusion.4 = f32[2,1024]{1,0:T(2,128)S(1)} fusion(f32[2,2048]{1,0:T(2,128)S(1)} %multiply_divide_fusion.1, f32[2,1024,2048]{2,1,0:T(8,128)} %get-tuple-element.21), kind=kLoop, calls=%fused_computation.10 | loop fusion | flops 12580864 | bytes 16801792 | tf_op jit(solution)/shard_map/reduce_sum | solution.py:57
  279.7 57.5 %all-reduce.1 = (f32[2,1024]{1,0:T(2,128)S(1)}, f32[2,1024]{1,0:T(2,128)S(1)}) all-reduce(f32[2,1024]{1,0:T(2,128)S(1)} %multiply_reduce_fusion.4, f32[2,1024]{1,0:T(2,128)S(1)} %get-tuple-element.6), channel_id=1, replica_groups=mesh['batch'=16,'proto'=16] {'proto'}, use_global_device_ids=true, to_apply=%region_15.0 | all-reduce | flops 4096 | bytes 32768 | tf_op jit(solution)/shard_map/psum | solution.py:23
  337.2 18.3 %fusion.2 = (f32[2,1024,2048]{2,1,0:T(8,128)}, f32[2,1024,2048]{2,1,0:T(8,128)}) fusion(f32[2,1024,2048]{2,1,0:T(8,128)} %get-tuple-element.21, f32[2,1024]{1,0:T(2,128)S(1)} %get-tuple-element.11, f32[2,1024]{1,0:T(2,128)S(1)} %get-tuple-element.10, f32[2,2048]{1,0:T(2,128)S(1)} %multiply_divide_fusion.1), kind=kLoop, calls=%fused_computation.11 | loop fusion | flops 20971520 | bytes 50364416 | tf_op jit(solution)/shard_map/div | solution.py:64
  355.5 19.2 %slice_subtract_fusion.1 = (f32[1,1024,2048]{2,1,0:T(8,128)}, f32[1,1024,2048]{2,1,0:T(8,128)}) fusion(f32[2,1024,2048]{2,1,0:T(8,128)} %get-tuple-element.17, f32[2,1024,2048]{2,1,0:T(8,128)} %get-tuple-element.16), kind=kLoop, calls=%fused_computation.14 | loop fusion | flops 4194304 | bytes 50331648 | tf_op jit(solution)/shard_map/sub | solution.py:65
  374.8 7.4 fusion.11
  382.3 29.8 %collective-permute-done = f32[2,1024,256]{1,2,0:T(8,128)S(1)} collective-permute-done((f32[2,1024,256]{1,2,0:T(8,128)S(1)}, f32[2,1024,256]{1,2,0:T(8,128)S(1)}, u32[]{:S(2)}, u32[]{:S(2)}) %collective-permute-start) | collective-permute-done | bytes 2097184 | tf_op jit(solution)/shard_map/ppermute | solution.py:73
  412.6 40.4 %collective-permute-done.1 = f32[2,1024,256]{1,2,0:T(8,128)S(1)} collective-permute-done((f32[2,1024,256]{1,2,0:T(8,128)S(1)}, f32[2,1024,256]{1,2,0:T(8,128)S(1)}, u32[]{:S(2)}, u32[]{:S(2)}) %collective-permute-start.1) | collective-permute-done | bytes 2097184 | tf_op jit(solution)/shard_map/ppermute | solution.py:73
  453.6 26.0 %collective-permute-done.2 = f32[2,1024,256]{1,2,0:T(8,128)S(1)} collective-permute-done((f32[2,1024,256]{1,2,0:T(8,128)S(1)}, f32[2,1024,256]{1,2,0:T(8,128)S(1)}, u32[]{:S(2)}, u32[]{:S(2)}) %collective-permute-start.2) | collective-permute-done | bytes 2097184 | tf_op jit(solution)/shard_map/ppermute | solution.py:73
  481.4 7.7 %collective-permute-start.3 = (f32[2,1024,256]{1,2,0:T(8,128)}, f32[2,1024,256]{1,2,0:T(8,128)}, u32[]{:S(2)}, u32[]{:S(2)}) collective-permute-start(f32[2,1024,256]{1,2,0:T(8,128)} %add.67), channel_id=1, source_target_pairs={{0,8},{1,9},{2,10},{3,11},{4,12},{5,13},{6,14},{7,15},{8,0},{9,1},... | collective-permute-start | bytes 6291464 | tf_op jit(solution)/shard_map/ppermute | solution.py:73
  489.0 4.0 convolution_bitcast_fusion
  493.1 147.2 %all-reduce.4.cloned.1.call-done = f32[2048,256]{1,0:T(8,128)} async-done(((f32[2048,256]{1,0:T(8,128)}), f32[2048,256]{1,0:T(8,128)}) %all-reduce.4.cloned.1.call-update) | async-done | bytes 2097168 | tf_op jit(solution)/shard_map/psum | solution.py:69
  642.5 3.6 multiply_reduce_fusion.7
  646.8 6.6 multiply_reduce_fusion.5
  654.2 77.9 %all-reduce = (f32[]{:T(128)}, f32[]{:T(128)}) all-reduce(f32[]{:T(128)S(6)} %div.101, f32[]{:T(128)S(6)} %div.104), channel_id=1, replica_groups=mesh['batch'=16,'proto'=16] {'batch','proto'}, use_global_device_ids=true, to_apply=%region_19.0 | all-reduce | flops 2 | bytes 16 | tf_op jit(solution)/shard_map/psum | solution.py:27
  (39 shorter events, 18.0 us)
Async XLA Ops:
  7.2 633.1 %all-reduce.4.cloned.1.call-start = ((), (), s32[]{:S(2)}) async-start(), calls=%async_computation | async-start | bytes 4194304 | tf_op jit(solution)/shard_map/psum | solution.py:69
  355.5 19.3 %copy-start = (f32[2048,256]{1,0:T(8,128)S(1)}, f32[2048,256]{1,0:T(8,128)}, u32[]{:S(2)}) copy-start(f32[2048,256]{1,0:T(8,128)} %param.5) | copy-start | bytes 6291460
  374.7 114.3 %slice-start.2 = ((s8[8388608]{0:T(1024)(128)(4,1)}), s8[4194304]{0:T(1024)(128)(4,1)S(1)}, s32[]{:S(2)}) async-start(s8[8388608]{0:T(1024)(128)(4,1)} %bitcast.18), calls=%async_computation.3 | async-start | bytes 8388608
  374.7 114.3 %slice-start.3 = ((s8[8388608]{0:T(1024)(128)(4,1)}), s8[4194304]{0:T(1024)(128)(4,1)S(1)}, s32[]{:S(2)}) async-start(s8[8388608]{0:T(1024)(128)(4,1)} %bitcast.18), calls=%async_computation.4 | async-start | bytes 8388608
  382.2 106.9 %slice-start = ((s8[8388608]{0:T(1024)(128)(4,1)}), s8[4194304]{0:T(1024)(128)(4,1)S(1)}, s32[]{:S(2)}) async-start(s8[8388608]{0:T(1024)(128)(4,1)} %bitcast.16), calls=%async_computation.1 | async-start | bytes 8388608
  382.2 29.9 %collective-permute-start = (f32[2,1024,256]{1,2,0:T(8,128)S(1)}, f32[2,1024,256]{1,2,0:T(8,128)S(1)}, u32[]{:S(2)}, u32[]{:S(2)}) collective-permute-start(f32[2,1024,256]{1,2,0:T(8,128)S(1)} %fusion.11), channel_id=1, source_target_pairs={{0,1},{1,0},{2,3},{3,2},{4,5},{5,4},{6,7},{7,6},{8,9},{9,8},{10,11... | collective-permute-start | bytes 6291464 | tf_op jit(solution)/shard_map/ppermute | solution.py:73
  412.5 76.5 %slice-start.1 = ((s8[8388608]{0:T(1024)(128)(4,1)}), s8[4194304]{0:T(1024)(128)(4,1)S(1)}, s32[]{:S(2)}) async-start(s8[8388608]{0:T(1024)(128)(4,1)} %bitcast.16), calls=%async_computation.2 | async-start | bytes 8388608
  412.5 40.5 %collective-permute-start.1 = (f32[2,1024,256]{1,2,0:T(8,128)S(1)}, f32[2,1024,256]{1,2,0:T(8,128)S(1)}, u32[]{:S(2)}, u32[]{:S(2)}) collective-permute-start(f32[2,1024,256]{1,2,0:T(8,128)S(1)} %add.65), channel_id=1, source_target_pairs={{0,2},{1,3},{2,0},{3,1},{4,6},{5,7},{6,4},{7,5},{8,10},{9,11},{10,... | collective-permute-start | bytes 6291464 | tf_op jit(solution)/shard_map/ppermute | solution.py:73
  453.5 26.1 %collective-permute-start.2 = (f32[2,1024,256]{1,2,0:T(8,128)S(1)}, f32[2,1024,256]{1,2,0:T(8,128)S(1)}, u32[]{:S(2)}, u32[]{:S(2)}) collective-permute-start(f32[2,1024,256]{1,2,0:T(8,128)S(1)} %add.66), channel_id=1, source_target_pairs={{0,4},{1,5},{2,6},{3,7},{4,0},{5,1},{6,2},{7,3},{8,12},{9,13},{10,... | collective-permute-start | bytes 6291464 | tf_op jit(solution)/shard_map/ppermute | solution.py:73
  481.4 165.4 %collective-permute-start.3 = (f32[2,1024,256]{1,2,0:T(8,128)}, f32[2,1024,256]{1,2,0:T(8,128)}, u32[]{:S(2)}, u32[]{:S(2)}) collective-permute-start(f32[2,1024,256]{1,2,0:T(8,128)} %add.67), channel_id=1, source_target_pairs={{0,8},{1,9},{2,10},{3,11},{4,12},{5,13},{6,14},{7,15},{8,0},{9,1},... | collective-permute-start | bytes 6291464 | tf_op jit(solution)/shard_map/ppermute | solution.py:73
  653.4 86.7 %copy-start.1 = (f32[2048,256]{1,0:T(8,128)S(1)}, f32[2048,256]{1,0:T(8,128)}, u32[]{:S(2)}) copy-start(f32[2048,256]{1,0:T(8,128)} %get-tuple-element.13) | copy-start | bytes 6291460
Sparse Core Ops, SparseCore 0:
  493.2 146.9 all-reduce.3
